TPU v7x, 32 devices: a whole 2x2x4 slice. The times are simulated.
32 devices in a mesh: rows: 4 (over y, x), cols: 8 (over z, core).
Axes of the slice: x: 2, y: 2, z: 4, core: 2. Of those that a mesh axis runs over, the one named last changes fastest.
Arguments:
- anomalies: float32 [16384, 1024], P('rows', 'cols'), may hold values from -75 to 75
- pairing: int32 [2, 8], replicated, may hold values from 0 to 7, as said below
Outputs:
- rotated: float32 [16384, 1024], P('rows', 'cols')
Inputs may be any that keep to these rules, and one draw needn't show every extreme that they name: pairing[r, b] = b XOR m_r with one m_r for the whole row r; m_0 is neither 0 nor 1024 // 128 - 1, and for odd r m_r is m_0 with every bit of 7 flipped, for even r it is m_0.
All inputs are finite; a program needn't handle non-finite values.
Results may differ from a plain program's by a relative error of at most 0.0003.
Values sent between devices are 32-bit elements; how exact they have to be, the bound alone decides.
A program may use at most 128 MiB of HBM per device.

v0:
```python
from functools import partial

import jax
import jax.numpy as jnp
from jax import lax
from jax.experimental import pallas as pl
from jax.experimental.pallas import tpu as pltpu
from jax.sharding import PartitionSpec as P

SHIFTS = 8
TIE_GUARD = 1e-06
MESH = pl.DeviceIdType.MESH
HIGHEST = lax.Precision.HIGHEST


def dot(left, right):
    return jnp.dot(left, right, precision=HIGHEST, preferred_element_type=jnp.float32)


def dot_t(left, right):
    return lax.dot_general(
        left,
        right,
        (((0,), (0,)), ((), ())),
        precision=HIGHEST,
        preferred_element_type=jnp.float32,
    )


def exchange_kernel(count, x_ref, out_ref, send_sem, recv_sem, local_sem):
    me = lax.axis_index("cols")
    chips = count // 2
    chip = me // 2
    core = me % 2
    side = 1 - 2 * (chip // (chips // 2))

    barrier = pltpu.get_barrier_semaphore()
    for d in range(1, count):
        pl.semaphore_signal(
            barrier, inc=1, device_id={"cols": (me + d) % count}, device_id_type=MESH
        )
    local = pltpu.make_async_copy(x_ref.at[me], out_ref.at[me], local_sem)
    local.start()
    pl.semaphore_wait(barrier, count - 1)

    copies = []
    for k in [*range(1, chips), 0]:
        for flip in (0, 1):
            if k == 0 and flip == 0:
                continue
            dest_chip = (chip + side * k + chips) % chips
            dest = dest_chip * 2 + (core + flip) % 2
            copy = pltpu.make_async_remote_copy(
                src_ref=x_ref.at[dest],
                dst_ref=out_ref.at[me],
                send_sem=send_sem.at[len(copies)],
                recv_sem=recv_sem.at[me],
                device_id={"cols": dest},
                device_id_type=MESH,
            )
            copy.start()
            copies.append(copy)
    local.wait()
    for d in range(1, count):
        source = (me + d) % count
        pltpu.make_async_remote_copy(
            src_ref=x_ref.at[source],
            dst_ref=out_ref.at[source],
            send_sem=send_sem.at[0],
            recv_sem=recv_sem.at[source],
            device_id={"cols": source},
            device_id_type=MESH,
        ).wait_recv()
    for copy in copies:
        copy.wait_send()


def exchange(x, collective_id):
    count = x.shape[0]
    return pl.pallas_call(
        partial(exchange_kernel, count),
        out_shape=jax.ShapeDtypeStruct(x.shape, x.dtype),
        in_specs=[pl.BlockSpec(memory_space=pl.ANY)],
        out_specs=pl.BlockSpec(memory_space=pl.ANY),
        scratch_shapes=[
            pltpu.SemaphoreType.DMA((count - 1,)),
            pltpu.SemaphoreType.DMA((count,)),
            pltpu.SemaphoreType.DMA,
        ],
        compiler_params=pltpu.CompilerParams(
            collective_id=collective_id, has_side_effects=True
        ),
    )(x)


def quad_blocks(pairing, count):
    m0 = pairing[0, 0]
    m1 = pairing[1, 0]
    lower_mask = jnp.minimum(m0, m1)
    low_bits = jnp.int32(0)
    for bit in range(1, count.bit_length() - 1):
        low_bits = jnp.where(lower_mask >= (1 << bit), (1 << bit) - 1, low_bits)
    g = jnp.arange(count // 4, dtype=jnp.int32)
    rest = g & low_bits
    q0 = rest + 2 * (g - rest)
    return jnp.stack([q0, q0 ^ m0, q0 ^ m1, q0 ^ (count - 1)], axis=1)


def gram_kernel(quads, x_ref, gram_ref):
    g = pl.program_id(0)
    a = jnp.concatenate([x_ref[quads[g, 0]], x_ref[quads[g, 1]]], axis=1)
    b = jnp.concatenate([x_ref[quads[g, 2]], x_ref[quads[g, 3]]], axis=1)
    gram_ref[0, 0] = dot_t(a, a)
    gram_ref[0, 1] = dot_t(b, b)
    gram_ref[0, 2] = dot_t(a, b)


def gram(quads, x):
    groups = quads.shape[0]
    width = 2 * x.shape[2]
    return pl.pallas_call(
        gram_kernel,
        grid_spec=pltpu.PrefetchScalarGridSpec(
            num_scalar_prefetch=1,
            grid=(groups,),
            in_specs=[pl.BlockSpec(memory_space=pltpu.VMEM)],
            out_specs=pl.BlockSpec((1, 3, width, width), lambda g, q: (g, 0, 0, 0)),
        ),
        out_shape=jax.ShapeDtypeStruct((groups, 3, width, width), jnp.float32),
    )(quads, x)


def turn_pairs(work):
    w = work.shape[2]
    row = lax.broadcasted_iota(jnp.int32, (w, w), 0)
    col = lax.broadcasted_iota(jnp.int32, (w, w), 1)

    def diag(value):
        return jnp.sum(jnp.where(row == col, value, 0.0), axis=0, keepdims=True)

    @pl.loop(0, SHIFTS)
    def _(step):
        for p in range(2):
            g_ll, g_lr, g_rl, g_rr = (work[p, i] for i in range(4))
            a, e, g = diag(g_ll), diag(g_rr), diag(g_lr)
            gap = e - a
            sign = jnp.where(gap >= 0.0, 1.0, -1.0)
            denom = jnp.abs(gap) + jnp.sqrt(gap * gap + 4.0 * g * g) + TIE_GUARD * (a + e)
            tangent = 2.0 * g * sign / denom
            cosine = 1.0 / jnp.sqrt(1.0 + tangent * tangent)
            sine = cosine * tangent
            cc = jnp.broadcast_to(cosine, (w, w))
            ss = jnp.broadcast_to(sine, (w, w))
            rc = cc.T
            rs = ss.T
            ul = g_ll * cc - g_lr * ss
            ll = g_rl * cc - g_rr * ss
            work[p, 0] = rc * ul - rs * ll
            work[p, 2] = pltpu.roll(rs * ul + rc * ll, w - 1, 0)
            ur = g_ll * ss + g_lr * cc
            lr = g_rl * ss + g_rr * cc
            work[p, 1] = pltpu.roll(rc * ur - rs * lr, w - 1, 1)
            work[p, 3] = pltpu.roll(pltpu.roll(rs * ur + rc * lr, w - 1, 0), w - 1, 1)
            for i in (4, 6):
                v_l, v_r = work[p, i], work[p, i + 1]
                work[p, i] = v_l * cc - v_r * ss
                work[p, i + 1] = pltpu.roll(v_l * ss + v_r * cc, w - 1, 1)


def rotate_kernel(gram_ref, turn_ref, work):
    w = work.shape[2]
    eye = jnp.where(
        lax.broadcasted_iota(jnp.int32, (w, w), 0) == lax.broadcasted_iota(jnp.int32, (w, w), 1),
        1.0,
        0.0,
    )
    lo, hi = slice(0, w), slice(w, 2 * w)

    def reset_turns():
        for p in range(2):
            work[p, 4] = eye
            work[p, 5] = jnp.zeros_like(eye)
            work[p, 6] = jnp.zeros_like(eye)
            work[p, 7] = eye

    def put_turns(p, slot):
        turn_ref[0, slot, lo, lo] = work[p, 4]
        turn_ref[0, slot, lo, hi] = pltpu.roll(work[p, 5], SHIFTS, 1)
        turn_ref[0, slot, hi, lo] = work[p, 6]
        turn_ref[0, slot, hi, hi] = pltpu.roll(work[p, 7], SHIFTS, 1)

    for p in range(2):
        work[p, 0] = gram_ref[0, p, lo, lo]
        work[p, 1] = gram_ref[0, p, lo, hi]
        work[p, 2] = gram_ref[0, p, hi, lo]
        work[p, 3] = gram_ref[0, p, hi, hi]
    reset_turns()
    turn_pairs(work)
    for p in range(2):
        put_turns(p, p)

    half = dot(gram_ref[0, 2], turn_ref[0, 1])
    cross = [
        dot_t(turn_ref[0, 0, :, lo], half[:, lo]),
        dot_t(turn_ref[0, 0, :, hi], half[:, hi]),
    ]
    left = [work[0, 0], pltpu.roll(pltpu.roll(work[0, 3], SHIFTS, 0), SHIFTS, 1)]
    right = [work[1, 0], pltpu.roll(pltpu.roll(work[1, 3], SHIFTS, 0), SHIFTS, 1)]
    for p in range(2):
        work[p, 0] = left[p]
        work[p, 1] = cross[p]
        work[p, 2] = cross[p].T
        work[p, 3] = right[p]
    reset_turns()
    turn_pairs(work)
    for p in range(2):
        put_turns(p, 2 + p)


def rotate(gram_sum):
    groups, _, width, _ = gram_sum.shape
    return pl.pallas_call(
        rotate_kernel,
        grid=(groups,),
        in_specs=[pl.BlockSpec((1, 3, width, width), lambda g: (g, 0, 0, 0))],
        out_specs=pl.BlockSpec((1, 4, width, width), lambda g: (g, 0, 0, 0)),
        out_shape=jax.ShapeDtypeStruct((groups, 4, width, width), jnp.float32),
        scratch_shapes=[pltpu.VMEM((2, 8, width // 2, width // 2), jnp.float32)],
    )(gram_sum)


def apply_kernel(quads, x_ref, turn_ref, y_ref):
    g = pl.program_id(0)
    w = x_ref.shape[2]
    q = [quads[g, i] for i in range(4)]
    a = dot(jnp.concatenate([x_ref[q[0]], x_ref[q[1]]], axis=1), turn_ref[0, 0])
    b = dot(jnp.concatenate([x_ref[q[2]], x_ref[q[3]]], axis=1), turn_ref[0, 1])
    c = dot(jnp.concatenate([a[:, :w], b[:, :w]], axis=1), turn_ref[0, 2])
    d = dot(jnp.concatenate([a[:, w:], b[:, w:]], axis=1), turn_ref[0, 3])
    y_ref[q[0]] = c[:, :w]
    y_ref[q[2]] = c[:, w:]
    y_ref[q[1]] = d[:, :w]
    y_ref[q[3]] = d[:, w:]


def apply_turns(quads, x, turns):
    groups, _, width, _ = turns.shape
    return pl.pallas_call(
        apply_kernel,
        grid_spec=pltpu.PrefetchScalarGridSpec(
            num_scalar_prefetch=1,
            grid=(groups,),
            in_specs=[
                pl.BlockSpec(memory_space=pltpu.VMEM),
                pl.BlockSpec((1, 4, width, width), lambda g, q: (g, 0, 0, 0)),
            ],
            out_specs=pl.BlockSpec(memory_space=pltpu.VMEM),
        ),
        out_shape=jax.ShapeDtypeStruct(x.shape, x.dtype),
    )(quads, x, turns)


def on_device(anomalies, pairing):
    count = lax.axis_size("cols")
    rows, width = anomalies.shape
    quads = quad_blocks(pairing, count)
    x = exchange(anomalies.reshape(count, rows // count, width), 1)
    gram_sum = lax.psum(gram(quads, x), ("rows", "cols"))
    turns = rotate(gram_sum)
    y = apply_turns(quads, x, turns)
    return exchange(y, 2).reshape(rows, width)


def solution(mesh):
    placed = (P("rows", "cols"), P())
    return jax.shard_map(
        on_device, mesh=mesh, in_specs=placed, out_specs=P("rows", "cols"), check_vma=False
    )
```

profile of v0, /device:TPU:0, one launch (start us, length us, event | category | flops | bytes accessed | tf_op | source)
XLA Modules:
  0.0 286.8 jit_solution(8489730879765992536)
XLA Ops:
  6.5 0.0 all-reduce.2.cloned.1.call-start
  6.5 1.3 fusion
  9.1 1.3 broadcast_xor_fusion.1
  10.4 51.6 %shard_map.28.x_ref = f32[8,512,128]{2,1,0:T(8,128)} custom-call(f32[8,512,128]{2,1,0:T(8,128)} %bitcast.5), custom_call_target="tpu_custom_call" | custom-call | tf_op jit(solution)/shard_map/pallas_call | solution.py:80
  62.0 0.7 pad_add_fusion.quads
  62.6 6.3 %shard_map.29 = f32[2,3,256,256]{3,2,1,0:T(8,128)} custom-call(s32[2,4]{1,0:T(2,128)} %pad_add_fusion.quads, f32[8,512,128]{2,1,0:T(8,128)} %shard_map.28.x_ref), custom_call_target="tpu_custom_call" | custom-call | tf_op jit(solution)/shard_map/pallas_call | solution.py:121
  68.9 0.0 all-reduce.2.cloned.1.call-update
  68.9 132.8 %all-reduce.2.cloned.1.call-done.gram_ref = f32[2,3,256,256]{3,2,1,0:T(8,128)} async-done(((f32[2,3,256,256]{3,2,1,0:T(8,128)}), f32[2,3,256,256]{3,2,1,0:T(8,128)}) %all-reduce.2.cloned.1.call-update) | async-done | bytes 1572880 | tf_op jit(solution)/shard_map/psum | solution.py:268
  201.8 18.5 %shard_map.30.turn_ref = f32[2,4,256,256]{3,2,1,0:T(8,128)} custom-call(f32[2,3,256,256]{3,2,1,0:T(8,128)} %all-reduce.2.cloned.1.call-done.gram_ref), custom_call_target="tpu_custom_call" | custom-call | tf_op jit(solution)/shard_map/pallas_call | solution.py:222
  220.2 8.0 %shard_map.31.x_ref = f32[8,512,128]{2,1,0:T(8,128)} custom-call(s32[2,4]{1,0:T(2,128)} %pad_add_fusion.quads, f32[8,512,128]{2,1,0:T(8,128)} %shard_map.28.x_ref, f32[2,4,256,256]{3,2,1,0:T(8,128)} %shard_map.30.turn_ref), custom_call_target="tpu_custom_call" | custom-call | tf_op jit(solution)/shard_map/pallas_call | solution.py:248
  228.2 48.7 %shard_map.32 = f32[8,512,128]{2,1,0:T(8,128)} custom-call(f32[8,512,128]{2,1,0:T(8,128)} %shard_map.31.x_ref), custom_call_target="tpu_custom_call" | custom-call | tf_op jit(solution)/shard_map/pallas_call | solution.py:80
  276.9 3.0 %copy.5 = f32[4096,128]{1,0:T(8,128)} copy(f32[4096,128]{1,0:T(8,128)} %bitcast.4) | data formatting | bytes 4194304
  (1 shorter events, 0.0 us)
Async XLA Ops:
  6.5 195.3 %all-reduce.2.cloned.1.call-start = ((), (), s32[]{:S(2)}) async-start(), calls=%async_computation | async-start | bytes 3145728 | tf_op jit(solution)/shard_map/psum | solution.py:268
Sparse Core Ops, SparseCore 0:
  69.1 132.6 all-reduce.1
where the time goes:
time: 287 us
  Pallas kernels  133 us (46%)
  waiting for transfers between devices  133 us (46%)
  between operations  14.7 us (5%)
  local copies, waits for them, and re-layouts  4.34 us (2%)
    psum x1, waiting for transfers between devices, on_device(): gram_sum = lax.psum(gram(quads, x), ('rows', 'cols'))  133 us
    pallas_call x2, Pallas kernels, exchange(): pl.pallas_call(partial(exchange_kernel, count), out_shape=jax.ShapeDtypeS...  100 us
    pallas_call x1, Pallas kernels, rotate(): pl.pallas_call(rotate_kernel, grid=(groups,), in_specs=[pl.BlockSpec((1,...  18.5 us
    pallas_call x1, Pallas kernels, apply_turns(): pl.pallas_call(apply_kernel, grid_spec=pltpu.PrefetchScalarGridSpec(num_s...  7.97 us
    pallas_call x1, Pallas kernels, gram(): pl.pallas_call(gram_kernel, grid_spec=pltpu.PrefetchScalarGridSpec(num_sc...  6.3 us
  transfers between devices with their start and end apart: 1, of which 1 were waited for; matrix products, arithmetic and copies ran while one was open for 0% of the time, Pallas kernels for 0%

commit v1 on v0

--- a/solution.py
+++ b/solution.py
@@ -9,6 +9,8 @@
 
 SHIFTS = 8
 TIE_GUARD = 1e-06
+BAND = 2 * SHIFTS
+PAIRS = 10
 MESH = pl.DeviceIdType.MESH
 HIGHEST = lax.Precision.HIGHEST
 
@@ -106,28 +108,129 @@
     return jnp.stack([q0, q0 ^ m0, q0 ^ m1, q0 ^ (count - 1)], axis=1)
 
 
-def gram_kernel(quads, x_ref, gram_ref):
+def lane_bit(shape, bit):
+    return (lax.broadcasted_iota(jnp.int32, shape, 1) & (1 << bit)) != 0
+
+
+def to_bands(block):
+    w = block.shape[0]
+    for bit in range(w.bit_length() - 1):
+        block = jnp.where(
+            lane_bit(block.shape, bit), pltpu.roll(block, w - (1 << bit), 0), block
+        )
+    return jnp.concatenate([block[w - BAND :], block[:BAND]], axis=0)
+
+
+def from_bands(bands):
+    w = bands.shape[1]
+    block = jnp.concatenate(
+        [bands[BAND:], jnp.zeros((w - 2 * BAND, w), jnp.float32), bands[:BAND]], axis=0
+    )
+    for bit in range(w.bit_length() - 1):
+        block = jnp.where(lane_bit(block.shape, bit), pltpu.roll(block, 1 << bit, 0), block)
+    return block
+
+
+def gram_kernel(quads, x_ref, band_ref):
     g = pl.program_id(0)
+    w = x_ref.shape[2]
+    lo, hi = slice(0, w), slice(w, 2 * w)
     a = jnp.concatenate([x_ref[quads[g, 0]], x_ref[quads[g, 1]]], axis=1)
     b = jnp.concatenate([x_ref[quads[g, 2]], x_ref[quads[g, 3]]], axis=1)
-    gram_ref[0, 0] = dot_t(a, a)
-    gram_ref[0, 1] = dot_t(b, b)
-    gram_ref[0, 2] = dot_t(a, b)
-
-
-def gram(quads, x):
-    groups = quads.shape[0]
-    width = 2 * x.shape[2]
+    aa, bb, ba = dot_t(a, a), dot_t(b, b), dot_t(b, a)
+    blocks = [aa[lo, lo], aa[hi, lo], aa[hi, hi], bb[lo, lo], bb[hi, lo], bb[hi, hi]]
+    blocks += [ba[lo, lo], ba[lo, hi], ba[hi, lo], ba[hi, hi]]
+
+    @pl.when(g == 0)
+    def _():
+        band_ref[...] = jnp.zeros_like(band_ref)
+
+    for i, block in enumerate(blocks):
+        start = pl.multiple_of((g * PAIRS + i) * 2 * BAND, 2 * BAND)
+        band_ref[pl.ds(start, 2 * BAND), :] = to_bands(block)
+
+
+def gram(quads, x, total):
     return pl.pallas_call(
         gram_kernel,
         grid_spec=pltpu.PrefetchScalarGridSpec(
             num_scalar_prefetch=1,
-            grid=(groups,),
+            grid=(quads.shape[0],),
             in_specs=[pl.BlockSpec(memory_space=pltpu.VMEM)],
-            out_specs=pl.BlockSpec((1, 3, width, width), lambda g, q: (g, 0, 0, 0)),
+            out_specs=pl.BlockSpec(memory_space=pltpu.VMEM),
         ),
-        out_shape=jax.ShapeDtypeStruct((groups, 3, width, width), jnp.float32),
+        out_shape=jax.ShapeDtypeStruct((total, x.shape[2]), jnp.float32),
     )(quads, x)
+
+
+def sum_kernel(x_ref, out_ref, landed, part, slots, whole, send_sem, recv_sem):
+    rows, cols = x_ref.shape[0], x_ref.shape[1]
+    r, c = lax.axis_index("rows"), lax.axis_index("cols")
+    barrier = pltpu.get_barrier_semaphore()
+    for d in range(1, rows):
+        pl.semaphore_signal(barrier, inc=1, device_id={"rows": (r + d) % rows}, device_id_type=MESH)
+    for d in range(1, cols):
+        pl.semaphore_signal(barrier, inc=1, device_id={"cols": (c + d) % cols}, device_id_type=MESH)
+    pl.semaphore_wait(barrier, rows + cols - 2)
+
+    def stage(number, axis, me, count, source, dest):
+        copies = []
+        for d in range(1, count):
+            peer = (me + d) % count
+            copy = pltpu.make_async_remote_copy(
+                src_ref=source(peer),
+                dst_ref=dest(d),
+                send_sem=send_sem.at[number, d],
+                recv_sem=recv_sem.at[number, d],
+                device_id={axis: peer},
+                device_id_type=MESH,
+            )
+            copy.start()
+            copies.append(copy)
+        for copy in copies:
+            copy.wait_recv()
+        return copies
+
+    def finish(copies):
+        for copy in copies:
+            copy.wait_send()
+
+    sent = stage(0, "rows", r, rows, lambda p: x_ref.at[p], lambda d: landed.at[d])
+    total = x_ref[r]
+    for d in range(1, rows):
+        total = total + landed[d]
+    part[...] = total
+    sent += stage(1, "cols", c, cols, lambda p: part.at[p], lambda d: slots.at[d])
+    total = part[c]
+    for d in range(1, cols):
+        total = total + slots[d]
+    whole[c] = total
+    sent += stage(2, "cols", c, cols, lambda p: whole.at[c], lambda d: whole.at[c])
+    out_ref[r] = whole[...]
+    sent += stage(3, "rows", r, rows, lambda p: whole, lambda d: out_ref.at[r])
+    finish(sent)
+
+
+def sum_all(x, rows, cols):
+    total, width = x.shape
+    piece = total // (rows * cols)
+    peers = max(rows, cols)
+    summed = pl.pallas_call(
+        sum_kernel,
+        out_shape=jax.ShapeDtypeStruct((rows, cols, piece, width), jnp.float32),
+        in_specs=[pl.BlockSpec(memory_space=pltpu.VMEM)],
+        out_specs=pl.BlockSpec(memory_space=pltpu.VMEM),
+        scratch_shapes=[
+            pltpu.VMEM((rows, cols, piece, width), jnp.float32),
+            pltpu.VMEM((cols, piece, width), jnp.float32),
+            pltpu.VMEM((cols, piece, width), jnp.float32),
+            pltpu.VMEM((cols, piece, width), jnp.float32),
+            pltpu.SemaphoreType.DMA((4, peers)),
+            pltpu.SemaphoreType.DMA((4, peers)),
+        ],
+        compiler_params=pltpu.CompilerParams(collective_id=3, has_side_effects=True),
+    )(x.reshape(rows, cols, piece, width))
+    return summed.reshape(total, width)
 
 
 def turn_pairs(work):
@@ -167,7 +270,7 @@
                 work[p, i + 1] = pltpu.roll(v_l * ss + v_r * cc, w - 1, 1)
 
 
-def rotate_kernel(gram_ref, turn_ref, work):
+def rotate_kernel(band_ref, turn_ref, work):
     w = work.shape[2]
     eye = jnp.where(
         lax.broadcasted_iota(jnp.int32, (w, w), 0) == lax.broadcasted_iota(jnp.int32, (w, w), 1),
@@ -175,6 +278,9 @@
         0.0,
     )
     lo, hi = slice(0, w), slice(w, 2 * w)
+
+    def block(i):
+        return from_bands(band_ref[i * 2 * BAND : (i + 1) * 2 * BAND, :])
 
     def reset_turns():
         for p in range(2):
@@ -190,26 +296,34 @@
         turn_ref[0, slot, hi, hi] = pltpu.roll(work[p, 7], SHIFTS, 1)
 
     for p in range(2):
-        work[p, 0] = gram_ref[0, p, lo, lo]
-        work[p, 1] = gram_ref[0, p, lo, hi]
-        work[p, 2] = gram_ref[0, p, hi, lo]
-        work[p, 3] = gram_ref[0, p, hi, hi]
+        work[p, 0] = block(3 * p)
+        below = block(3 * p + 1)
+        work[p, 1] = below.T
+        work[p, 2] = below
+        work[p, 3] = block(3 * p + 2)
     reset_turns()
     turn_pairs(work)
     for p in range(2):
         put_turns(p, p)
 
-    half = dot(gram_ref[0, 2], turn_ref[0, 1])
-    cross = [
-        dot_t(turn_ref[0, 0, :, lo], half[:, lo]),
-        dot_t(turn_ref[0, 0, :, hi], half[:, hi]),
+    cross = jnp.concatenate(
+        [
+            jnp.concatenate([block(6), block(7)], axis=1),
+            jnp.concatenate([block(8), block(9)], axis=1),
+        ],
+        axis=0,
+    )
+    half = dot(cross, turn_ref[0, 0])
+    below = [
+        dot_t(turn_ref[0, 1, :, lo], half[:, lo]),
+        dot_t(turn_ref[0, 1, :, hi], half[:, hi]),
     ]
     left = [work[0, 0], pltpu.roll(pltpu.roll(work[0, 3], SHIFTS, 0), SHIFTS, 1)]
     right = [work[1, 0], pltpu.roll(pltpu.roll(work[1, 3], SHIFTS, 0), SHIFTS, 1)]
     for p in range(2):
         work[p, 0] = left[p]
-        work[p, 1] = cross[p]
-        work[p, 2] = cross[p].T
+        work[p, 1] = below[p].T
+        work[p, 2] = below[p]
         work[p, 3] = right[p]
     reset_turns()
     turn_pairs(work)
@@ -217,16 +331,16 @@
         put_turns(p, 2 + p)
 
 
-def rotate(gram_sum):
-    groups, _, width, _ = gram_sum.shape
+def rotate(bands, groups):
+    w = bands.shape[1]
     return pl.pallas_call(
         rotate_kernel,
         grid=(groups,),
-        in_specs=[pl.BlockSpec((1, 3, width, width), lambda g: (g, 0, 0, 0))],
-        out_specs=pl.BlockSpec((1, 4, width, width), lambda g: (g, 0, 0, 0)),
-        out_shape=jax.ShapeDtypeStruct((groups, 4, width, width), jnp.float32),
-        scratch_shapes=[pltpu.VMEM((2, 8, width // 2, width // 2), jnp.float32)],
-    )(gram_sum)
+        in_specs=[pl.BlockSpec((PAIRS * 2 * BAND, w), lambda g: (g, 0))],
+        out_specs=pl.BlockSpec((1, 4, 2 * w, 2 * w), lambda g: (g, 0, 0, 0)),
+        out_shape=jax.ShapeDtypeStruct((groups, 4, 2 * w, 2 * w), jnp.float32),
+        scratch_shapes=[pltpu.VMEM((2, 8, w, w), jnp.float32)],
+    )(bands)
 
 
 def apply_kernel(quads, x_ref, turn_ref, y_ref):
@@ -265,8 +379,12 @@
     rows, width = anomalies.shape
     quads = quad_blocks(pairing, count)
     x = exchange(anomalies.reshape(count, rows // count, width), 1)
-    gram_sum = lax.psum(gram(quads, x), ("rows", "cols"))
-    turns = rotate(gram_sum)
+    split = lax.axis_size("rows")
+    groups = count // 4
+    unit = 8 * split * count
+    total = -(-groups * PAIRS * 2 * BAND // unit) * unit
+    bands = sum_all(gram(quads, x, total), split, count)
+    turns = rotate(bands, groups)
     y = apply_turns(quads, x, turns)
     return exchange(y, 2).reshape(rows, width)
 

time: 287 us -> 167 us (0.58)
  waiting for transfers between devices: 133 us -> 0 us
  Pallas kernels: 133 us -> 159 us
  between operations: 14.7 us -> 1.33 us
    psum x1 -> x0, waiting for transfers between devices: 133 us -> none  [on_device(): gram_sum = lax.psum(gram(quads, x), ('rows', 'cols'))]
    pallas_call x1 -> x2, Pallas kernels: 18.5 us -> 44.5 us  [the longest x1 26 us: sum_all(): pl.pallas_call(sum_kernel, out_shape=jax.ShapeDtypeStruct((rows, cols, pi...]
  transfers between devices with their start and end apart: 1 -> 0, of which waited for: 1 -> 0; matrix products, arithmetic and copies ran while one was open for 0% -> 0% of each run, Pallas kernels for 0% -> 0%
where the time goes in v1:
time: 167 us
  Pallas kernels  159 us (95%)
  local copies, waits for them, and re-layouts  4.37 us (3%)
  other arithmetic  1.97 us (1%)
    pallas_call x2, Pallas kernels, exchange(): pl.pallas_call(partial(exchange_kernel, count), out_shape=jax.ShapeDtypeS...  100 us
    pallas_call x1, Pallas kernels, sum_all(): pl.pallas_call(sum_kernel, out_shape=jax.ShapeDtypeStruct((rows, cols, pi...  26 us
    pallas_call x1, Pallas kernels, rotate(): pl.pallas_call(rotate_kernel, grid=(groups,), in_specs=[pl.BlockSpec((PAI...  18.5 us
    pallas_call x1, Pallas kernels, apply_turns(): pl.pallas_call(apply_kernel, grid_spec=pltpu.PrefetchScalarGridSpec(num_s...  7.96 us
    pallas_call x1, Pallas kernels, gram(): pl.pallas_call(gram_kernel, grid_spec=pltpu.PrefetchScalarGridSpec(num_sc...  6.69 us

profile of v1, /device:TPU:0, one launch (start us, length us, event | category | flops | bytes accessed | tf_op | source)
XLA Modules:
  0.0 167.0 jit_solution(12169033838892113628)
XLA Ops:
  0.0 1.3 fusion
  2.6 1.3 broadcast_xor_fusion.1
  3.9 0.7 pad_add_fusion.quads
  4.6 51.4 %shard_map.28.x_ref = f32[8,512,128]{2,1,0:T(8,128)} custom-call(f32[8,512,128]{2,1,0:T(8,128)} %bitcast.7), custom_call_target="tpu_custom_call" | custom-call | tf_op jit(solution)/shard_map/pallas_call | solution.py:82
  56.1 6.7 %shard_map.29 = f32[768,128]{1,0:T(8,128)} custom-call(s32[2,4]{1,0:T(2,128)} %pad_add_fusion.quads, f32[8,512,128]{2,1,0:T(8,128)} %shard_map.28.x_ref), custom_call_target="tpu_custom_call" | custom-call | tf_op jit(solution)/shard_map/pallas_call | solution.py:154
  62.7 26.0 %shard_map.30 = f32[4,8,24,128]{3,2,1,0:T(8,128)} custom-call(f32[4,8,24,128]{3,2,1,0:T(8,128)} %bitcast.9), custom_call_target="tpu_custom_call" | custom-call | tf_op jit(solution)/shard_map/pallas_call | solution.py:218
  88.7 18.5 %shard_map.31.turn_ref = f32[2,4,256,256]{3,2,1,0:T(8,128)} custom-call(f32[768,128]{1,0:T(8,128)} %bitcast.8), custom_call_target="tpu_custom_call" | custom-call | tf_op jit(solution)/shard_map/pallas_call | solution.py:336
  107.3 8.0 %shard_map.32.x_ref = f32[8,512,128]{2,1,0:T(8,128)} custom-call(s32[2,4]{1,0:T(2,128)} %pad_add_fusion.quads, f32[8,512,128]{2,1,0:T(8,128)} %shard_map.28.x_ref, f32[2,4,256,256]{3,2,1,0:T(8,128)} %shard_map.31.turn_ref), custom_call_target="tpu_custom_call" | custom-call | tf_op jit(solution)/shard_map/pallas_call | solution.py:362
  115.2 48.7 %shard_map.33 = f32[8,512,128]{2,1,0:T(8,128)} custom-call(f32[8,512,128]{2,1,0:T(8,128)} %shard_map.32.x_ref), custom_call_target="tpu_custom_call" | custom-call | tf_op jit(solution)/shard_map/pallas_call | solution.py:82
  164.0 3.0 %copy.4 = f32[4096,128]{1,0:T(8,128)} copy(f32[4096,128]{1,0:T(8,128)} %bitcast.6) | data formatting | bytes 4194304
  (1 shorter events, 0.0 us)

commit v2 on v1

--- a/solution.py
+++ b/solution.py
@@ -95,17 +95,16 @@
     )(x)
 
 
-def quad_blocks(pairing, count):
+def quad_blocks(pairing, count, g):
     m0 = pairing[0, 0]
     m1 = pairing[1, 0]
     lower_mask = jnp.minimum(m0, m1)
     low_bits = jnp.int32(0)
     for bit in range(1, count.bit_length() - 1):
         low_bits = jnp.where(lower_mask >= (1 << bit), (1 << bit) - 1, low_bits)
-    g = jnp.arange(count // 4, dtype=jnp.int32)
     rest = g & low_bits
     q0 = rest + 2 * (g - rest)
-    return jnp.stack([q0, q0 ^ m0, q0 ^ m1, q0 ^ (count - 1)], axis=1)
+    return q0, q0 ^ m0, q0 ^ m1, q0 ^ (count - 1)
 
 
 def lane_bit(shape, bit):
@@ -131,12 +130,13 @@
     return block
 
 
-def gram_kernel(quads, x_ref, band_ref):
+def gram_kernel(pairing, x_ref, band_ref):
     g = pl.program_id(0)
+    q = quad_blocks(pairing, x_ref.shape[0], g)
     w = x_ref.shape[2]
     lo, hi = slice(0, w), slice(w, 2 * w)
-    a = jnp.concatenate([x_ref[quads[g, 0]], x_ref[quads[g, 1]]], axis=1)
-    b = jnp.concatenate([x_ref[quads[g, 2]], x_ref[quads[g, 3]]], axis=1)
+    a = jnp.concatenate([x_ref[q[0]], x_ref[q[1]]], axis=1)
+    b = jnp.concatenate([x_ref[q[2]], x_ref[q[3]]], axis=1)
     aa, bb, ba = dot_t(a, a), dot_t(b, b), dot_t(b, a)
     blocks = [aa[lo, lo], aa[hi, lo], aa[hi, hi], bb[lo, lo], bb[hi, lo], bb[hi, hi]]
     blocks += [ba[lo, lo], ba[lo, hi], ba[hi, lo], ba[hi, hi]]
@@ -150,17 +150,17 @@
         band_ref[pl.ds(start, 2 * BAND), :] = to_bands(block)
 
 
-def gram(quads, x, total):
+def gram(pairing, x, total):
     return pl.pallas_call(
         gram_kernel,
         grid_spec=pltpu.PrefetchScalarGridSpec(
             num_scalar_prefetch=1,
-            grid=(quads.shape[0],),
+            grid=(x.shape[0] // 4,),
             in_specs=[pl.BlockSpec(memory_space=pltpu.VMEM)],
             out_specs=pl.BlockSpec(memory_space=pltpu.VMEM),
         ),
         out_shape=jax.ShapeDtypeStruct((total, x.shape[2]), jnp.float32),
-    )(quads, x)
+    )(pairing, x)
 
 
 def sum_kernel(x_ref, out_ref, landed, part, slots, whole, send_sem, recv_sem):
@@ -233,120 +233,132 @@
     return summed.reshape(total, width)
 
 
-def turn_pairs(work):
-    w = work.shape[2]
-    row = lax.broadcasted_iota(jnp.int32, (w, w), 0)
-    col = lax.broadcasted_iota(jnp.int32, (w, w), 1)
-
-    def diag(value):
-        return jnp.sum(jnp.where(row == col, value, 0.0), axis=0, keepdims=True)
+def turn_pairs(gram, turn, pairs):
+    _, depth, sides, w = gram.shape
+
+    def lane(value):
+        return pltpu.roll(value.reshape(depth * sides, w), w - 1, 1).reshape(depth, sides, w)
+
+    def later(value):
+        return jnp.concatenate([value[-1:], value[:-1]], axis=0)
+
+    def sooner(value):
+        return jnp.concatenate([value[1:], value[:1]], axis=0)
+
+    def swap(value):
+        return jnp.concatenate([value[:, pairs:], value[:, :pairs]], axis=1)
+
+    def ahead(value):
+        return jnp.stack([pltpu.roll(value, (BAND - r) % w, 1) if r != BAND else value for r in range(depth)])
+
+    lower = lax.broadcasted_iota(jnp.int32, (depth, sides, w), 1) >= pairs
 
     @pl.loop(0, SHIFTS)
     def _(step):
+        g_l, g_r = gram[0], gram[1]
+        a, e, g = gram[0, BAND, :pairs], gram[1, BAND, pairs:], gram[1, BAND, :pairs]
+        gap = e - a
+        sign = jnp.where(gap >= 0.0, 1.0, -1.0)
+        denom = jnp.abs(gap) + jnp.sqrt(gap * gap + 4.0 * g * g) + TIE_GUARD * (a + e)
+        tangent = 2.0 * g * sign / denom
+        cosine = 1.0 / jnp.sqrt(1.0 + tangent * tangent)
+        sine = cosine * tangent
+        c_2 = jnp.concatenate([cosine, cosine], axis=0)
+        s_2 = jnp.concatenate([sine, sine], axis=0)
+        c_d = ahead(c_2)
+        s_d = ahead(jnp.concatenate([-sine, sine], axis=0))
+        t_l = g_l * c_2 - g_r * s_2
+        t_r = g_l * s_2 + g_r * c_2
+        t_l = c_d * t_l + s_d * swap(t_l)
+        t_r = lane(c_d * t_r + s_d * swap(t_r))
+        gram[0] = jnp.where(lower, sooner(t_l), t_l)
+        gram[1] = jnp.where(lower, t_r, later(t_r))
+        v_l, v_r = turn[0], turn[1]
+        turn[0] = v_l * c_2 - v_r * s_2
+        turn[1] = later(lane(v_l * s_2 + v_r * c_2))
+
+
+def rotate_kernel(groups, band_ref, turn_ref, gram, turn):
+    w = band_ref.shape[1]
+    pairs = 2 * groups
+    lo, hi = slice(0, w), slice(w, 2 * w)
+
+    def bands(g, i):
+        start = (g * PAIRS + i) * 2 * BAND
+        return band_ref[start : start + 2 * BAND, :]
+
+    def reset_turns():
+        shape = turn.shape
+        one = lax.broadcasted_iota(jnp.int32, shape, 1) == BAND
+        lower = lax.broadcasted_iota(jnp.int32, shape, 2) >= pairs
+        right = lax.broadcasted_iota(jnp.int32, shape, 0) == 1
+        turn[...] = jnp.where(one & (lower == right), 1.0, 0.0)
+
+    def put_turns(slot):
+        for g in range(groups):
+            for p in range(2):
+                at = 2 * g + p
+                for row, side in ((lo, at), (hi, pairs + at)):
+                    turn_ref[g, slot + p, row, lo] = from_bands(turn[0, :, side, :])
+                    moved = from_bands(turn[1, :, side, :])
+                    turn_ref[g, slot + p, row, hi] = pltpu.roll(moved, SHIFTS, 1)
+
+    def put_gram(at, ll, lr, rl, rr):
+        gram[0, :, at, :] = ll
+        gram[1, :, at, :] = lr
+        gram[0, :, pairs + at, :] = rl
+        gram[1, :, pairs + at, :] = rr
+
+    for g in range(groups):
         for p in range(2):
-            g_ll, g_lr, g_rl, g_rr = (work[p, i] for i in range(4))
-            a, e, g = diag(g_ll), diag(g_rr), diag(g_lr)
-            gap = e - a
-            sign = jnp.where(gap >= 0.0, 1.0, -1.0)
-            denom = jnp.abs(gap) + jnp.sqrt(gap * gap + 4.0 * g * g) + TIE_GUARD * (a + e)
-            tangent = 2.0 * g * sign / denom
-            cosine = 1.0 / jnp.sqrt(1.0 + tangent * tangent)
-            sine = cosine * tangent
-            cc = jnp.broadcast_to(cosine, (w, w))
-            ss = jnp.broadcast_to(sine, (w, w))
-            rc = cc.T
-            rs = ss.T
-            ul = g_ll * cc - g_lr * ss
-            ll = g_rl * cc - g_rr * ss
-            work[p, 0] = rc * ul - rs * ll
-            work[p, 2] = pltpu.roll(rs * ul + rc * ll, w - 1, 0)
-            ur = g_ll * ss + g_lr * cc
-            lr = g_rl * ss + g_rr * cc
-            work[p, 1] = pltpu.roll(rc * ur - rs * lr, w - 1, 1)
-            work[p, 3] = pltpu.roll(pltpu.roll(rs * ur + rc * lr, w - 1, 0), w - 1, 1)
-            for i in (4, 6):
-                v_l, v_r = work[p, i], work[p, i + 1]
-                work[p, i] = v_l * cc - v_r * ss
-                work[p, i + 1] = pltpu.roll(v_l * ss + v_r * cc, w - 1, 1)
-
-
-def rotate_kernel(band_ref, turn_ref, work):
-    w = work.shape[2]
-    eye = jnp.where(
-        lax.broadcasted_iota(jnp.int32, (w, w), 0) == lax.broadcasted_iota(jnp.int32, (w, w), 1),
-        1.0,
-        0.0,
-    )
-    lo, hi = slice(0, w), slice(w, 2 * w)
-
-    def block(i):
-        return from_bands(band_ref[i * 2 * BAND : (i + 1) * 2 * BAND, :])
-
-    def reset_turns():
-        for p in range(2):
-            work[p, 4] = eye
-            work[p, 5] = jnp.zeros_like(eye)
-            work[p, 6] = jnp.zeros_like(eye)
-            work[p, 7] = eye
-
-    def put_turns(p, slot):
-        turn_ref[0, slot, lo, lo] = work[p, 4]
-        turn_ref[0, slot, lo, hi] = pltpu.roll(work[p, 5], SHIFTS, 1)
-        turn_ref[0, slot, hi, lo] = work[p, 6]
-        turn_ref[0, slot, hi, hi] = pltpu.roll(work[p, 7], SHIFTS, 1)
-
-    for p in range(2):
-        work[p, 0] = block(3 * p)
-        below = block(3 * p + 1)
-        work[p, 1] = below.T
-        work[p, 2] = below
-        work[p, 3] = block(3 * p + 2)
+            below = bands(g, 3 * p + 1)
+            above = to_bands(from_bands(below).T)
+            put_gram(2 * g + p, bands(g, 3 * p), above, below, bands(g, 3 * p + 2))
     reset_turns()
-    turn_pairs(work)
-    for p in range(2):
-        put_turns(p, p)
-
-    cross = jnp.concatenate(
-        [
-            jnp.concatenate([block(6), block(7)], axis=1),
-            jnp.concatenate([block(8), block(9)], axis=1),
-        ],
-        axis=0,
-    )
-    half = dot(cross, turn_ref[0, 0])
-    below = [
-        dot_t(turn_ref[0, 1, :, lo], half[:, lo]),
-        dot_t(turn_ref[0, 1, :, hi], half[:, hi]),
-    ]
-    left = [work[0, 0], pltpu.roll(pltpu.roll(work[0, 3], SHIFTS, 0), SHIFTS, 1)]
-    right = [work[1, 0], pltpu.roll(pltpu.roll(work[1, 3], SHIFTS, 0), SHIFTS, 1)]
-    for p in range(2):
-        work[p, 0] = left[p]
-        work[p, 1] = below[p].T
-        work[p, 2] = below[p]
-        work[p, 3] = right[p]
+    turn_pairs(gram, turn, pairs)
+    put_turns(0)
+
+    for g in range(groups):
+        blocks = [from_bands(bands(g, 6 + i)) for i in range(4)]
+        cross = jnp.concatenate(
+            [
+                jnp.concatenate([blocks[0], blocks[1]], axis=1),
+                jnp.concatenate([blocks[2], blocks[3]], axis=1),
+            ],
+            axis=0,
+        )
+        half = dot(cross, turn_ref[g, 0])
+        below = [
+            dot_t(turn_ref[g, 1, :, lo], half[:, lo]),
+            dot_t(turn_ref[g, 1, :, hi], half[:, hi]),
+        ]
+        a, b = 2 * g, 2 * g + 1
+        a_lo, b_lo = gram[0, :, a, :], gram[0, :, b, :]
+        a_hi = pltpu.roll(gram[1, :, pairs + a, :], SHIFTS, 1)
+        b_hi = pltpu.roll(gram[1, :, pairs + b, :], SHIFTS, 1)
+        put_gram(a, a_lo, to_bands(below[0].T), to_bands(below[0]), b_lo)
+        put_gram(b, a_hi, to_bands(below[1].T), to_bands(below[1]), b_hi)
     reset_turns()
-    turn_pairs(work)
-    for p in range(2):
-        put_turns(p, 2 + p)
+    turn_pairs(gram, turn, pairs)
+    put_turns(2)
 
 
 def rotate(bands, groups):
     w = bands.shape[1]
+    state = pltpu.VMEM((2, 2 * BAND, 4 * groups, w), jnp.float32)
     return pl.pallas_call(
-        rotate_kernel,
-        grid=(groups,),
-        in_specs=[pl.BlockSpec((PAIRS * 2 * BAND, w), lambda g: (g, 0))],
-        out_specs=pl.BlockSpec((1, 4, 2 * w, 2 * w), lambda g: (g, 0, 0, 0)),
+        partial(rotate_kernel, groups),
+        in_specs=[pl.BlockSpec(memory_space=pltpu.VMEM)],
+        out_specs=pl.BlockSpec(memory_space=pltpu.VMEM),
         out_shape=jax.ShapeDtypeStruct((groups, 4, 2 * w, 2 * w), jnp.float32),
-        scratch_shapes=[pltpu.VMEM((2, 8, w, w), jnp.float32)],
+        scratch_shapes=[state, state],
     )(bands)
 
 
-def apply_kernel(quads, x_ref, turn_ref, y_ref):
+def apply_kernel(pairing, x_ref, turn_ref, y_ref):
     g = pl.program_id(0)
     w = x_ref.shape[2]
-    q = [quads[g, i] for i in range(4)]
+    q = quad_blocks(pairing, x_ref.shape[0], g)
     a = dot(jnp.concatenate([x_ref[q[0]], x_ref[q[1]]], axis=1), turn_ref[0, 0])
     b = dot(jnp.concatenate([x_ref[q[2]], x_ref[q[3]]], axis=1), turn_ref[0, 1])
     c = dot(jnp.concatenate([a[:, :w], b[:, :w]], axis=1), turn_ref[0, 2])
@@ -357,7 +369,7 @@
     y_ref[q[3]] = d[:, w:]
 
 
-def apply_turns(quads, x, turns):
+def apply_turns(pairing, x, turns):
     groups, _, width, _ = turns.shape
     return pl.pallas_call(
         apply_kernel,
@@ -371,21 +383,20 @@
             out_specs=pl.BlockSpec(memory_space=pltpu.VMEM),
         ),
         out_shape=jax.ShapeDtypeStruct(x.shape, x.dtype),
-    )(quads, x, turns)
+    )(pairing, x, turns)
 
 
 def on_device(anomalies, pairing):
     count = lax.axis_size("cols")
     rows, width = anomalies.shape
-    quads = quad_blocks(pairing, count)
     x = exchange(anomalies.reshape(count, rows // count, width), 1)
     split = lax.axis_size("rows")
     groups = count // 4
     unit = 8 * split * count
     total = -(-groups * PAIRS * 2 * BAND // unit) * unit
-    bands = sum_all(gram(quads, x, total), split, count)
+    bands = sum_all(gram(pairing, x, total), split, count)
     turns = rotate(bands, groups)
-    y = apply_turns(quads, x, turns)
+    y = apply_turns(pairing, x, turns)
     return exchange(y, 2).reshape(rows, width)
 
 

time: 167 us -> 154 us (0.922)
  Pallas kernels: 159 us -> 151 us
  other arithmetic: 1.97 us -> 0 us
    pallas_call x1, Pallas kernels: 18.5 us -> 9.91 us  [rotate(): pl.pallas_call(partial(rotate_kernel, groups), in_specs=[pl.BlockSpec(mem...]
where the time goes in v2:
time: 154 us
  Pallas kernels  151 us (98%)
  local copies, waits for them, and re-layouts  3.05 us (2%)
    pallas_call x2, Pallas kernels, exchange(): pl.pallas_call(partial(exchange_kernel, count), out_shape=jax.ShapeDtypeS...  100 us
    pallas_call x1, Pallas kernels, sum_all(): pl.pallas_call(sum_kernel, out_shape=jax.ShapeDtypeStruct((rows, cols, pi...  26 us
    pallas_call x1, Pallas kernels, rotate(): pl.pallas_call(partial(rotate_kernel, groups), in_specs=[pl.BlockSpec(mem...  9.91 us
    pallas_call x1, Pallas kernels, apply_turns(): pl.pallas_call(apply_kernel, grid_spec=pltpu.PrefetchScalarGridSpec(num_s...  7.95 us
    pallas_call x1, Pallas kernels, gram(): pl.pallas_call(gram_kernel, grid_spec=pltpu.PrefetchScalarGridSpec(num_sc...  6.7 us

profile of v2, /device:TPU:0, one launch (start us, length us, event | category | flops | bytes accessed | tf_op | source)
XLA Modules:
  0.0 153.8 jit_solution(7316516637048730455)
XLA Ops:
  0.0 51.4 %shard_map.28.x_ref = f32[8,512,128]{2,1,0:T(8,128)} custom-call(f32[8,512,128]{2,1,0:T(8,128)} %bitcast.5), custom_call_target="tpu_custom_call" | custom-call | tf_op jit(solution)/shard_map/pallas_call | solution.py:82
  51.5 6.7 %shard_map.29 = f32[768,128]{1,0:T(8,128)} custom-call(s32[2,8]{1,0:T(2,128)} %pairing.3, f32[8,512,128]{2,1,0:T(8,128)} %shard_map.28.x_ref), custom_call_target="tpu_custom_call" | custom-call | tf_op jit(solution)/shard_map/pallas_call | solution.py:154
  58.2 26.0 %shard_map.30 = f32[4,8,24,128]{3,2,1,0:T(8,128)} custom-call(f32[4,8,24,128]{3,2,1,0:T(8,128)} %bitcast.7), custom_call_target="tpu_custom_call" | custom-call | tf_op jit(solution)/shard_map/pallas_call | solution.py:218
  84.2 9.9 %shard_map.31.turn_ref = f32[2,4,256,256]{3,2,1,0:T(8,128)} custom-call(f32[768,128]{1,0:T(8,128)} %bitcast.6), custom_call_target="tpu_custom_call" | custom-call | tf_op jit(solution)/shard_map/pallas_call | solution.py:349
  94.1 8.0 %shard_map.32.x_ref = f32[8,512,128]{2,1,0:T(8,128)} custom-call(s32[2,8]{1,0:T(2,128)} %pairing.3, f32[8,512,128]{2,1,0:T(8,128)} %shard_map.28.x_ref, f32[2,4,256,256]{3,2,1,0:T(8,128)} %shard_map.31.turn_ref), custom_call_target="tpu_custom_call" | custom-call | tf_op jit(solution)/shard_map/pallas_call | solution.py:374
  102.0 48.7 %shard_map.33 = f32[8,512,128]{2,1,0:T(8,128)} custom-call(f32[8,512,128]{2,1,0:T(8,128)} %shard_map.32.x_ref), custom_call_target="tpu_custom_call" | custom-call | tf_op jit(solution)/shard_map/pallas_call | solution.py:82
  150.8 3.0 %copy.4 = f32[4096,128]{1,0:T(8,128)} copy(f32[4096,128]{1,0:T(8,128)} %bitcast.4) | data formatting | bytes 4194304

commit v3 on v2

--- a/solution.py
+++ b/solution.py
@@ -29,7 +29,7 @@
     )
 
 
-def exchange_kernel(count, x_ref, out_ref, send_sem, recv_sem, local_sem):
+def exchange_kernel(count, make_piece, out_ref, send_sem, recv_sem, local_sem):
     me = lax.axis_index("cols")
     chips = count // 2
     chip = me // 2
@@ -41,10 +41,6 @@
         pl.semaphore_signal(
             barrier, inc=1, device_id={"cols": (me + d) % count}, device_id_type=MESH
         )
-    local = pltpu.make_async_copy(x_ref.at[me], out_ref.at[me], local_sem)
-    local.start()
-    pl.semaphore_wait(barrier, count - 1)
-
     copies = []
     for k in [*range(1, chips), 0]:
         for flip in (0, 1):
@@ -52,8 +48,11 @@
                 continue
             dest_chip = (chip + side * k + chips) % chips
             dest = dest_chip * 2 + (core + flip) % 2
+            piece = make_piece(len(copies), dest)
+            if not copies:
+                pl.semaphore_wait(barrier, count - 1)
             copy = pltpu.make_async_remote_copy(
-                src_ref=x_ref.at[dest],
+                src_ref=piece,
                 dst_ref=out_ref.at[me],
                 send_sem=send_sem.at[len(copies)],
                 recv_sem=recv_sem.at[me],
@@ -62,11 +61,13 @@
             )
             copy.start()
             copies.append(copy)
+    local = pltpu.make_async_copy(make_piece(count - 1, me), out_ref.at[me], local_sem)
+    local.start()
     local.wait()
     for d in range(1, count):
         source = (me + d) % count
         pltpu.make_async_remote_copy(
-            src_ref=x_ref.at[source],
+            src_ref=copies[0].src_ref,
             dst_ref=out_ref.at[source],
             send_sem=send_sem.at[0],
             recv_sem=recv_sem.at[source],
@@ -77,18 +78,65 @@
         copy.wait_send()
 
 
+def gather_kernel(count, x_ref, out_ref, *sems):
+    exchange_kernel(count, lambda i, dest: x_ref.at[dest], out_ref, *sems)
+
+
+def halves(value):
+    high = value.astype(jnp.bfloat16)
+    return high, (value - high.astype(jnp.float32)).astype(jnp.bfloat16)
+
+
+def dot_3(left, right):
+    a, b = halves(left)
+    c, d = halves(right)
+    product = partial(jnp.dot, preferred_element_type=jnp.float32)
+    return product(a, c) + (product(a, d) + product(b, c))
+
+
+def return_kernel(count, pairing, x_ref, coef_ref, out_ref, piece_ref, *sems):
+    masks = (pairing[0, 0], pairing[1, 0], count - 1)
+
+    def make_piece(i, dest):
+        blocks = [x_ref[dest]] + [x_ref[dest ^ mask] for mask in masks]
+        piece_ref[i] = dot_3(jnp.concatenate(blocks, axis=1), coef_ref[dest])
+        return piece_ref.at[i]
+
+    exchange_kernel(count, make_piece, out_ref, *sems)
+
+
+def exchange_sems(count):
+    return [
+        pltpu.SemaphoreType.DMA((count - 1,)),
+        pltpu.SemaphoreType.DMA((count,)),
+        pltpu.SemaphoreType.DMA,
+    ]
+
+
+def turn_and_return(pairing, x, coef):
+    count = x.shape[0]
+    return pl.pallas_call(
+        partial(return_kernel, count),
+        out_shape=jax.ShapeDtypeStruct(x.shape, x.dtype),
+        in_specs=[
+            pl.BlockSpec(memory_space=pltpu.SMEM),
+            pl.BlockSpec(memory_space=pltpu.VMEM),
+            pl.BlockSpec(memory_space=pltpu.VMEM),
+        ],
+        out_specs=pl.BlockSpec(memory_space=pl.ANY),
+        scratch_shapes=[pltpu.VMEM(x.shape, x.dtype), *exchange_sems(count)],
+        compiler_params=pltpu.CompilerParams(collective_id=2, has_side_effects=True),
+    )(pairing, x, coef)
+
+
 def exchange(x, collective_id):
     count = x.shape[0]
     return pl.pallas_call(
-        partial(exchange_kernel, count),
+        partial(gather_kernel, count),
         out_shape=jax.ShapeDtypeStruct(x.shape, x.dtype),
         in_specs=[pl.BlockSpec(memory_space=pl.ANY)],
         out_specs=pl.BlockSpec(memory_space=pl.ANY),
-        scratch_shapes=[
-            pltpu.SemaphoreType.DMA((count - 1,)),
-            pltpu.SemaphoreType.DMA((count,)),
-            pltpu.SemaphoreType.DMA,
-        ],
+        scratch_shapes=exchange_sems(count),
         compiler_params=pltpu.CompilerParams(
             collective_id=collective_id, has_side_effects=True
         ),
@@ -278,7 +326,7 @@
         turn[1] = later(lane(v_l * s_2 + v_r * c_2))
 
 
-def rotate_kernel(groups, band_ref, turn_ref, gram, turn):
+def rotate_kernel(groups, pairing, band_ref, coef_ref, turn_ref, gram, turn):
     w = band_ref.shape[1]
     pairs = 2 * groups
     lo, hi = slice(0, w), slice(w, 2 * w)
@@ -342,48 +390,35 @@
     turn_pairs(gram, turn, pairs)
     put_turns(2)
 
-
-def rotate(bands, groups):
+    for g in range(groups):
+        q = quad_blocks(pairing, 4 * groups, g)
+        for side, part in ((0, lo), (1, hi)):
+            last = turn_ref.at[g, 2 + side]
+            top = dot(turn_ref[g, 0, :, part], last[lo, :])
+            bottom = dot(turn_ref[g, 1, :, part], last[hi, :])
+            rows = [top[lo], top[hi], bottom[lo], bottom[hi]]
+            for member, cols in ((side, lo), (2 + side, hi)):
+                for i in range(4):
+                    coef_ref[q[member], i * w : (i + 1) * w, :] = rows[member ^ i][:, cols]
+
+
+def rotate(pairing, bands, groups):
     w = bands.shape[1]
     state = pltpu.VMEM((2, 2 * BAND, 4 * groups, w), jnp.float32)
     return pl.pallas_call(
         partial(rotate_kernel, groups),
-        in_specs=[pl.BlockSpec(memory_space=pltpu.VMEM)],
+        in_specs=[
+            pl.BlockSpec(memory_space=pltpu.SMEM),
+            pl.BlockSpec(memory_space=pltpu.VMEM),
+        ],
         out_specs=pl.BlockSpec(memory_space=pltpu.VMEM),
-        out_shape=jax.ShapeDtypeStruct((groups, 4, 2 * w, 2 * w), jnp.float32),
-        scratch_shapes=[state, state],
-    )(bands)
-
-
-def apply_kernel(pairing, x_ref, turn_ref, y_ref):
-    g = pl.program_id(0)
-    w = x_ref.shape[2]
-    q = quad_blocks(pairing, x_ref.shape[0], g)
-    a = dot(jnp.concatenate([x_ref[q[0]], x_ref[q[1]]], axis=1), turn_ref[0, 0])
-    b = dot(jnp.concatenate([x_ref[q[2]], x_ref[q[3]]], axis=1), turn_ref[0, 1])
-    c = dot(jnp.concatenate([a[:, :w], b[:, :w]], axis=1), turn_ref[0, 2])
-    d = dot(jnp.concatenate([a[:, w:], b[:, w:]], axis=1), turn_ref[0, 3])
-    y_ref[q[0]] = c[:, :w]
-    y_ref[q[2]] = c[:, w:]
-    y_ref[q[1]] = d[:, :w]
-    y_ref[q[3]] = d[:, w:]
-
-
-def apply_turns(pairing, x, turns):
-    groups, _, width, _ = turns.shape
-    return pl.pallas_call(
-        apply_kernel,
-        grid_spec=pltpu.PrefetchScalarGridSpec(
-            num_scalar_prefetch=1,
-            grid=(groups,),
-            in_specs=[
-                pl.BlockSpec(memory_space=pltpu.VMEM),
-                pl.BlockSpec((1, 4, width, width), lambda g, q: (g, 0, 0, 0)),
-            ],
-            out_specs=pl.BlockSpec(memory_space=pltpu.VMEM),
-        ),
-        out_shape=jax.ShapeDtypeStruct(x.shape, x.dtype),
-    )(pairing, x, turns)
+        out_shape=jax.ShapeDtypeStruct((4 * groups, 4 * w, w), jnp.float32),
+        scratch_shapes=[
+            pltpu.VMEM((groups, 4, 2 * w, 2 * w), jnp.float32),
+            state,
+            state,
+        ],
+    )(pairing, bands)
 
 
 def on_device(anomalies, pairing):
@@ -395,9 +430,8 @@
     unit = 8 * split * count
     total = -(-groups * PAIRS * 2 * BAND // unit) * unit
     bands = sum_all(gram(pairing, x, total), split, count)
-    turns = rotate(bands, groups)
-    y = apply_turns(pairing, x, turns)
-    return exchange(y, 2).reshape(rows, width)
+    coef = rotate(pairing, bands, groups)
+    return turn_and_return(pairing, x, coef).reshape(rows, width)
 
 
 def solution(mesh):

time: 154 us -> 150 us (0.974)
  Pallas kernels: 151 us -> 147 us
    pallas_call x3 -> x2, Pallas kernels: 108 us -> 102 us  [the longest x1 51.4 us: exchange(): pl.pallas_call(partial(gather_kernel, count), out_shape=jax.ShapeDtypeStr...]
    pallas_call x1, Pallas kernels: 9.91 us -> 11.5 us  [rotate(): pl.pallas_call(partial(rotate_kernel, groups), in_specs=[pl.BlockSpec(mem...]
where the time goes in v3:
time: 150 us
  Pallas kernels  147 us (98%)
  local copies, waits for them, and re-layouts  3.05 us (2%)
    pallas_call x1, Pallas kernels, exchange(): pl.pallas_call(partial(gather_kernel, count), out_shape=jax.ShapeDtypeStr...  51.4 us
    pallas_call x1, Pallas kernels, turn_and_return(): pl.pallas_call(partial(return_kernel, count), out_shape=jax.ShapeDtypeStr...  50.8 us
    pallas_call x1, Pallas kernels, sum_all(): pl.pallas_call(sum_kernel, out_shape=jax.ShapeDtypeStruct((rows, cols, pi...  26 us
    pallas_call x1, Pallas kernels, rotate(): pl.pallas_call(partial(rotate_kernel, groups), in_specs=[pl.BlockSpec(mem...  11.5 us
    pallas_call x1, Pallas kernels, gram(): pl.pallas_call(gram_kernel, grid_spec=pltpu.PrefetchScalarGridSpec(num_sc...  6.7 us
    unnamed x1, local copies, waits for them, and re-layouts  3.05 us

profile of v3, /device:TPU:0, one launch (start us, length us, event | category | flops | bytes accessed | tf_op | source)
XLA Modules:
  0.0 149.6 jit_solution(8002069712005031115)
XLA Ops:
  0.0 51.4 %shard_map.28.x_ref = f32[8,512,128]{2,1,0:T(8,128)} custom-call(f32[8,512,128]{2,1,0:T(8,128)} %bitcast.5), custom_call_target="tpu_custom_call" | custom-call | tf_op jit(solution)/shard_map/pallas_call | solution.py:134
  51.5 6.7 %shard_map.29 = f32[768,128]{1,0:T(8,128)} custom-call(s32[2,8]{1,0:T(2,128)} %pairing.5, f32[8,512,128]{2,1,0:T(8,128)} %shard_map.28.x_ref), custom_call_target="tpu_custom_call" | custom-call | tf_op jit(solution)/shard_map/pallas_call | solution.py:202
  58.2 26.0 %shard_map.30 = f32[4,8,24,128]{3,2,1,0:T(8,128)} custom-call(f32[4,8,24,128]{3,2,1,0:T(8,128)} %bitcast.7), custom_call_target="tpu_custom_call" | custom-call | tf_op jit(solution)/shard_map/pallas_call | solution.py:266
  84.2 11.5 %shard_map.31.coef_ref = f32[8,512,128]{2,1,0:T(8,128)} custom-call(s32[2,8]{1,0:T(2,128)} %pairing.5, f32[768,128]{1,0:T(8,128)} %bitcast.6), custom_call_target="tpu_custom_call" | custom-call | tf_op jit(solution)/shard_map/pallas_call | solution.py:408
  95.7 50.8 %shard_map.32 = f32[8,512,128]{2,1,0:T(8,128)} custom-call(s32[2,8]{1,0:T(2,128)} %pairing.5, f32[8,512,128]{2,1,0:T(8,128)} %shard_map.28.x_ref, f32[8,512,128]{2,1,0:T(8,128)} %shard_map.31.coef_ref), custom_call_target="tpu_custom_call" | custom-call | tf_op jit(solution)/shard_map/pallas_call | solution.py:118
  146.5 3.0 %copy.4 = f32[4096,128]{1,0:T(8,128)} copy(f32[4096,128]{1,0:T(8,128)} %bitcast.4) | data formatting | bytes 4194304

commit v4 on v3

--- a/solution.py
+++ b/solution.py
@@ -178,13 +178,12 @@
     return block
 
 
-def gram_kernel(pairing, x_ref, band_ref):
+def gram_kernel(pairing, x_0, x_1, x_2, x_3, band_ref):
     g = pl.program_id(0)
-    q = quad_blocks(pairing, x_ref.shape[0], g)
-    w = x_ref.shape[2]
+    w = x_0.shape[2]
     lo, hi = slice(0, w), slice(w, 2 * w)
-    a = jnp.concatenate([x_ref[q[0]], x_ref[q[1]]], axis=1)
-    b = jnp.concatenate([x_ref[q[2]], x_ref[q[3]]], axis=1)
+    a = jnp.concatenate([x_0[0], x_1[0]], axis=1)
+    b = jnp.concatenate([x_2[0], x_3[0]], axis=1)
     aa, bb, ba = dot_t(a, a), dot_t(b, b), dot_t(b, a)
     blocks = [aa[lo, lo], aa[hi, lo], aa[hi, hi], bb[lo, lo], bb[hi, lo], bb[hi, hi]]
     blocks += [ba[lo, lo], ba[lo, hi], ba[hi, lo], ba[hi, hi]]
@@ -199,16 +198,23 @@
 
 
 def gram(pairing, x, total):
+    count = x.shape[0]
+
+    def member(i):
+        return pl.BlockSpec(
+            (1, *x.shape[1:]), lambda g, pairing: (quad_blocks(pairing, count, g)[i], 0, 0)
+        )
+
     return pl.pallas_call(
         gram_kernel,
         grid_spec=pltpu.PrefetchScalarGridSpec(
             num_scalar_prefetch=1,
-            grid=(x.shape[0] // 4,),
-            in_specs=[pl.BlockSpec(memory_space=pltpu.VMEM)],
+            grid=(count // 4,),
+            in_specs=[member(i) for i in range(4)],
             out_specs=pl.BlockSpec(memory_space=pltpu.VMEM),
         ),
         out_shape=jax.ShapeDtypeStruct((total, x.shape[2]), jnp.float32),
-    )(pairing, x)
+    )(pairing, x, x, x, x)
 
 
 def sum_kernel(x_ref, out_ref, landed, part, slots, whole, send_sem, recv_sem):

time: 150 us -> 149 us (level)
  no operation moved by 1% of the time
where the time goes in v4:
time: 149 us
  Pallas kernels  146 us (98%)
  local copies, waits for them, and re-layouts  3.05 us (2%)
    pallas_call x1, Pallas kernels, exchange(): pl.pallas_call(partial(gather_kernel, count), out_shape=jax.ShapeDtypeStr...  51.4 us
    pallas_call x1, Pallas kernels, turn_and_return(): pl.pallas_call(partial(return_kernel, count), out_shape=jax.ShapeDtypeStr...  50.8 us
    pallas_call x1, Pallas kernels, sum_all(): pl.pallas_call(sum_kernel, out_shape=jax.ShapeDtypeStruct((rows, cols, pi...  26 us
    pallas_call x1, Pallas kernels, rotate(): pl.pallas_call(partial(rotate_kernel, groups), in_specs=[pl.BlockSpec(mem...  11.5 us
    pallas_call x1, Pallas kernels, gram(): pl.pallas_call(gram_kernel, grid_spec=pltpu.PrefetchScalarGridSpec(num_sc...  6.34 us
    unnamed x1, local copies, waits for them, and re-layouts  3.05 us

profile of v4, /device:TPU:0, one launch (start us, length us, event | category | flops | bytes accessed | tf_op | source)
XLA Modules:
  0.0 149.2 jit_solution(1811254010712987690)
XLA Ops:
  0.0 51.4 %shard_map.28.x_0.x_1.x_2.x_3.x_ref = f32[8,512,128]{2,1,0:T(8,128)} custom-call(f32[8,512,128]{2,1,0:T(8,128)} %bitcast.5), custom_call_target="tpu_custom_call" | custom-call | tf_op jit(solution)/shard_map/pallas_call | solution.py:134
  51.5 6.3 %shard_map.29 = f32[768,128]{1,0:T(8,128)} custom-call(s32[2,8]{1,0:T(2,128)} %pairing.5, f32[8,512,128]{2,1,0:T(8,128)} %shard_map.28.x_0.x_1.x_2.x_3.x_ref, f32[8,512,128]{2,1,0:T(8,128)} %shard_map.28.x_0.x_1.x_2.x_3.x_ref, f32[8,512,128]{2,1,0:T(8,128)} %shard_map.28.x_0.x_1.x_2.x_3.x_ref, f32[8,512,128]{2,1,0:T(8,128)} %shard_map.28.x_0.x_1.x_2.x_3.x_ref), custom_call_target="tpu_custom_call" | custom-call | tf_op jit(solution)/shard_map/pallas_call | solution.py:208
  57.8 26.0 %shard_map.30 = f32[4,8,24,128]{3,2,1,0:T(8,128)} custom-call(f32[4,8,24,128]{3,2,1,0:T(8,128)} %bitcast.6), custom_call_target="tpu_custom_call" | custom-call | tf_op jit(solution)/shard_map/pallas_call | solution.py:272
  83.8 11.5 %shard_map.31.coef_ref = f32[8,512,128]{2,1,0:T(8,128)} custom-call(s32[2,8]{1,0:T(2,128)} %pairing.5, f32[768,128]{1,0:T(8,128)} %bitcast.7), custom_call_target="tpu_custom_call" | custom-call | tf_op jit(solution)/shard_map/pallas_call | solution.py:414
  95.3 50.8 %shard_map.32 = f32[8,512,128]{2,1,0:T(8,128)} custom-call(s32[2,8]{1,0:T(2,128)} %pairing.5, f32[8,512,128]{2,1,0:T(8,128)} %shard_map.28.x_0.x_1.x_2.x_3.x_ref, f32[8,512,128]{2,1,0:T(8,128)} %shard_map.31.coef_ref), custom_call_target="tpu_custom_call" | custom-call | tf_op jit(solution)/shard_map/pallas_call | solution.py:118
  146.2 3.0 %copy.4 = f32[4096,128]{1,0:T(8,128)} copy(f32[4096,128]{1,0:T(8,128)} %bitcast.4) | data formatting | bytes 4194304
